TPU v7x, 128 devices: a whole 4x4x4 slice. The times are simulated.
128 devices in a mesh: tiles: 128 (over x, z, y, core).
Axes of the slice: x: 4, y: 4, z: 4, core: 2. Of those that a mesh axis runs over, the one named last changes fastest.
Arguments:
- primal_start: float32 [256, 512, 1024], P('tiles'), may hold values from 0 to 1
- cost: bfloat16 [256, 512, 1024], P('tiles'), may hold values from -4 to 4
- mask: int32 [256, 64, 8], P('tiles'), may hold values 0 or 1
- tile_adv: int32 [256], P('tiles'), may hold values from -1 to 127, as said below
- tile_slot: int32 [256], P('tiles'), may hold values from -1 to 127
- adv_dual: float32 [128, 512], P('tiles'), may hold values from 0 to 2
- slot_dual: float32 [128, 1024], P('tiles'), may hold values from 0 to 2
- spend_limit: float32 [128, 512], P('tiles'), may hold values from 204 to 921
- capacity: float32 [128, 1024], P('tiles'), may hold values from 64 to 384
Outputs:
- primal: float32 [256, 512, 1024], P('tiles')
- adv_out: float32 [128, 512], P('tiles')
- slot_out: float32 [128, 1024], P('tiles')
Inputs may be any that keep to these rules, and one draw needn't show every extreme that they name: -1 marks an empty tile slot; tile_adv and tile_slot are -1 at the same slots. Each device's 2 slots hold 1 to 2 tiles, in its first slots, and some device holds exactly 2.
All inputs are finite; a program needn't handle non-finite values. No bound on the sum of `mask` on one device may be relied on, other than what follows from the above.
Results may differ from a plain program's by a relative error of at most 0.0003.
Values sent between devices are 32-bit elements; how exact they have to be, the bound alone decides.
No kernel may reach another device: no remote copies, remote signals or barrier semaphores. Data moves between devices by JAX's collectives and lax.ppermute only.
A program may use at most 64 MiB of HBM per device.

v0:
```python
import jax
import jax.numpy as jnp
from jax import lax
from jax.sharding import PartitionSpec as P

MB_ROWS = 8
MB_COLS = 128
ITERS = 2
tau_step = 0.5


def expand_mask(blocks, block_rows, block_cols):
    values = blocks.astype(jnp.float32)
    rows_in = values.shape[-2]
    cols_in = values.shape[-1]
    shaped = jnp.broadcast_to(
        values[..., :, None, :, None],
        values.shape[:-2] + (rows_in, block_rows, cols_in, block_cols),
    )
    return shaped.reshape(values.shape[:-2] + (rows_in * block_rows, cols_in * block_cols))


def body(primal_start, cost, mask, tile_adv, tile_slot, adv_dual, slot_dual, spend_limit, capacity):
    highest = lax.Precision.HIGHEST
    devices = lax.axis_size("tiles")
    adv_local = adv_dual.shape[0]
    slot_local = slot_dual.shape[0]
    rows_tile = primal_start.shape[1]
    cols_tile = primal_start.shape[2]
    adv_onehot = (
        tile_adv[:, None] == jnp.arange(adv_local * devices, dtype=jnp.int32)[None, :]
    ).astype(jnp.float32)
    slot_onehot = (
        tile_slot[:, None] == jnp.arange(slot_local * devices, dtype=jnp.int32)[None, :]
    ).astype(jnp.float32)
    present = (tile_adv >= 0).astype(jnp.float32)
    weight = expand_mask(mask, MB_ROWS, MB_COLS) * present[:, None, None]
    primal = weight * primal_start
    for sweep_index in range(ITERS):
        adv_all, slot_all = (
            lax.all_gather(adv_dual, "tiles", axis=0, tiled=True),
            lax.all_gather(slot_dual, "tiles", axis=0, tiled=True),
        )
        adv_rows = jnp.dot(adv_onehot, adv_all, precision=highest)
        slot_cols = jnp.dot(slot_onehot, slot_all, precision=highest)
        update = weight * jnp.clip(
            primal
            - tau_step * (cost.astype(jnp.float32) + adv_rows[:, :, None] + slot_cols[:, None, :]),
            0.0,
            1.0,
        )
        extended = 2.0 * update - primal
        row_blocks = jnp.dot(adv_onehot.T, jnp.sum(extended, axis=2), precision=highest)
        col_blocks = jnp.dot(slot_onehot.T, jnp.sum(extended, axis=1), precision=highest)
        primal, row_blocks, col_blocks = (update, row_blocks, col_blocks)
        row_mine, col_mine = (
            lax.psum_scatter(row_blocks, "tiles", scatter_dimension=0, tiled=True),
            lax.psum_scatter(col_blocks, "tiles", scatter_dimension=0, tiled=True),
        )
        adv_dual = jnp.maximum(adv_dual + (row_mine - spend_limit) / cols_tile, 0.0)
        slot_dual = jnp.maximum(slot_dual + (col_mine - capacity) / rows_tile, 0.0)
    return (primal, adv_dual, slot_dual)


def solution(mesh):
    return jax.shard_map(
        body,
        mesh=mesh,
        in_specs=(
            P("tiles", None, None),
            P("tiles", None, None),
            P("tiles", None, None),
            P("tiles"),
            P("tiles"),
            P("tiles", None),
            P("tiles", None),
            P("tiles", None),
            P("tiles", None),
        ),
        out_specs=(P("tiles", None, None), P("tiles", None), P("tiles", None)),
        check_vma=False,
    )
```

profile of v0, /device:TPU:1, one launch (start us, length us, event | category | flops | bytes accessed | tf_op | source)
XLA Modules:
  0.0 469.9 jit_solution(5772442257037595880)
XLA Ops:
  7.2 0.0 copy-start.3
  7.2 0.0 copy-start.4
  7.2 0.0 all-reduce.11.cloned.1.call-start
  7.2 0.7 compare_convert_fusion
  7.9 0.7 convert_element_type.12
  8.6 0.1 copy.13
  8.7 38.9 %all-gather = f32[128,1,512]{2,1,0:T(1,128)S(1)} all-gather(f32[1,1,512]{2,1,0:T(1,128)} %bitcast.50), channel_id=1, replica_groups=mesh['tiles'=128] {'tiles'}, dimensions={0}, use_global_device_ids=true | all-gather | bytes 264192 | tf_op jit(solution)/shard_map/all_gather | solution.py:41
  47.6 0.9 fusion.22
  48.4 33.9 %all-gather.1 = f32[128,1,1024]{2,1,0:T(1,128)S(1)} all-gather(f32[1,1,1024]{2,1,0:T(1,128)} %bitcast.49), channel_id=1, replica_groups=mesh['tiles'=128] {'tiles'}, dimensions={0}, use_global_device_ids=true | all-gather | bytes 528384 | tf_op jit(solution)/shard_map/all_gather | solution.py:42
  82.4 0.0 copy-start.5
  82.4 0.0 copy-start.6
  82.4 1.0 fusion.16
  83.4 0.0 copy-start.1
  83.4 0.0 copy-start.2
  83.4 0.0 copy-start
  83.4 5.0 %fusion.26 = (f32[2,512]{1,0:T(2,128)S(1)}, f32[2,1024]{1,0:T(2,128)S(1)}) fusion(f32[2,512,1024]{2,1,0:T(8,128)} %param.9, f32[2]{0:T(128)S(1)} %compare_convert_fusion, f32[2,64,8]{2,1,0:T(8,128)S(1)} %copy.13, f32[2,1024]{1,0:T(2,128)S(1)} %fusion.16, f32[2,512]{1,0:T(2,128)S(1)} %fusion.22, bf16[2,512,1024]{2,1,0:T(8,128)(2,1)} %param.10), kind=kLoop, calls=%fused_computation.31 | loop fusion | flops 13628416 | bytes 6320136 | tf_op jit(solution)/shard_map/reduce_sum | solution.py:53
  88.4 0.0 copy-done.3
  88.4 1.1 fusion.42
  89.5 0.0 copy-done.4
  89.5 1.3 fusion.40
  90.8 0.0 all-reduce.11.cloned.1.call-update
  90.8 0.0 all-reduce.9.cloned.1.call-start
  90.9 145.2 %all-reduce.11.cloned.1.call-done = (f32[128,1024]{1,0:T(8,128)}, f32[128,512]{1,0:T(8,128)}) async-done(((f32[128,1024]{1,0:T(8,128)}, f32[128,512]{1,0:T(8,128)}), (f32[128,1024]{1,0:T(8,128)}, f32[128,512]{1,0:T(8,128)})) %all-reduce.11.cloned.1.call-update) | async-done | bytes 786448
  236.0 0.0 copy-done.5
  236.0 0.0 copy-done.6
  236.0 0.7 fusion.37
  236.8 35.2 %all-gather.2 = f32[128,1,512]{2,1,0:T(1,128)S(1)} all-gather(f32[1,1,512]{2,1,0:T(1,128)S(1)} %bitcast.48), channel_id=1, replica_groups=mesh['tiles'=128] {'tiles'}, dimensions={0}, use_global_device_ids=true | all-gather | bytes 264192 | tf_op jit(solution)/shard_map/all_gather | solution.py:41
  272.0 0.2 fusion.19
  272.2 0.0 copy-done.1
  272.2 0.0 copy-done.2
  272.2 0.8 fusion.31
  273.0 34.0 %all-gather.3 = f32[128,1,1024]{2,1,0:T(1,128)S(1)} all-gather(f32[1,1,1024]{2,1,0:T(1,128)S(1)} %bitcast.47), channel_id=1, replica_groups=mesh['tiles'=128] {'tiles'}, dimensions={0}, use_global_device_ids=true | all-gather | bytes 528384 | tf_op jit(solution)/shard_map/all_gather | solution.py:42
  307.0 0.3 fusion.13
  307.3 0.0 copy-done
  307.3 6.4 %fusion.11 = (f32[2,1024]{1,0:T(2,128)S(1)}, f32[2,512]{1,0:T(2,128)S(1)}, f32[2,512,1024]{2,1,0:T(8,128)}) fusion(f32[2,1024]{1,0:T(2,128)S(1)} %fusion.16, f32[2,512]{1,0:T(2,128)S(1)} %fusion.22, bf16[2,512,1024]{2,1,0:T(8,128)(2,1)S(1)} %copy-done, f32[2,512,1024]{2,1,0:T(8,128)} %param.9, f32[2]{0:T(128)S(1)} %compare_convert_fusion, ...), kind=kLoop, calls=%fused_computation.16 | loop fusion | flops 19919872 | bytes 10526728 | tf_op jit(solution)/shard_map/reduce_sum | solution.py:54
  313.7 1.1 fusion.41
  314.8 1.3 fusion.39
  316.1 0.0 all-reduce.9.cloned.1.call-update
  316.1 144.2 %all-reduce.9.cloned.1.call-done = (f32[128,512]{1,0:T(8,128)}, f32[128,1024]{1,0:T(8,128)}) async-done(((f32[128,512]{1,0:T(8,128)}, f32[128,1024]{1,0:T(8,128)}), (f32[128,512]{1,0:T(8,128)}, f32[128,1024]{1,0:T(8,128)})) %all-reduce.9.cloned.1.call-update) | async-done | bytes 786448
  460.4 1.3 fusion.38
  461.7 1.4 fusion.32
Async XLA Ops:
  7.2 81.2 %copy-start.3 = (s32[2]{0:T(128)S(1)}, s32[2]{0:T(128)}, u32[]{:S(2)}) copy-start(s32[2]{0:T(128)} %param.12) | copy-start | bytes 28
  7.2 82.3 %copy-start.4 = (s32[2]{0:T(128)S(1)}, s32[2]{0:T(128)}, u32[]{:S(2)}) copy-start(s32[2]{0:T(128)} %param.13) | copy-start | bytes 28
  7.2 228.8 %all-reduce.11.cloned.1.call-start = ((), (), s32[]{:S(2)}) async-start(), calls=%async_computation.1 | async-start | bytes 1572864
  82.4 153.7 %copy-start.5 = (f32[1,512]{1,0:T(1,128)S(1)}, f32[1,512]{1,0:T(1,128)}, u32[]{:S(2)}) copy-start(f32[1,512]{1,0:T(1,128)} %param.14) | copy-start | bytes 6148
  82.4 153.7 %copy-start.6 = (f32[1,512]{1,0:T(1,128)S(1)}, f32[1,512]{1,0:T(1,128)}, u32[]{:S(2)}) copy-start(f32[1,512]{1,0:T(1,128)} %param.16) | copy-start | bytes 6148
  83.4 188.8 %copy-start.1 = (f32[1,1024]{1,0:T(1,128)S(1)}, f32[1,1024]{1,0:T(1,128)}, u32[]{:S(2)}) copy-start(f32[1,1024]{1,0:T(1,128)} %param.15) | copy-start | bytes 12292
  83.4 188.8 %copy-start.2 = (f32[1,1024]{1,0:T(1,128)S(1)}, f32[1,1024]{1,0:T(1,128)}, u32[]{:S(2)}) copy-start(f32[1,1024]{1,0:T(1,128)} %param.17) | copy-start | bytes 12292
  83.4 223.9 %copy-start = (bf16[2,512,1024]{2,1,0:T(8,128)(2,1)S(1)}, bf16[2,512,1024]{2,1,0:T(8,128)(2,1)}, u32[]{:S(2)}) copy-start(bf16[2,512,1024]{2,1,0:T(8,128)(2,1)} %param.10) | copy-start | bytes 6291460
  90.8 369.6 %all-reduce.9.cloned.1.call-start = ((), (), s32[]{:S(2)}) async-start(), calls=%async_computation | async-start | bytes 1572864
Sparse Core Ops, SparseCore 0:
  90.9 145.0 all-reduce.10
  316.2 144.0 all-reduce.8
where the time goes:
time: 471 us; the launch traced here: 470 us
  waiting for transfers between devices  289 us (61%)
  blocking collectives  142 us (30%)
  other arithmetic  16.9 us (4%)
  between operations  14.1 us (3%)
  matrix products  7.18 us (2%)
    unnamed x4, waiting for transfers between devices  289 us
    all_gather x2, blocking collectives, body(): lax.all_gather(adv_dual, 'tiles', axis=0, tiled=True)  74.1 us
    all_gather x2, blocking collectives, body(): lax.all_gather(slot_dual, 'tiles', axis=0, tiled=True)  67.9 us
  transfers between devices with their start and end apart: 2, of which 2 were waited for; matrix products, arithmetic and copies ran while one was open for 0% of the time, Pallas kernels for 0%

commit v1 on v0

--- a/solution.py
+++ b/solution.py
@@ -38,7 +38,10 @@
     primal = weight * primal_start
     for sweep_index in range(ITERS):
         adv_all, slot_all = (
-            lax.all_gather(adv_dual, "tiles", axis=0, tiled=True),
+            jnp.concatenate(
+                lax.all_to_all(jnp.stack([adv_dual] * lax.axis_size("tiles")), "tiles", 0, 0),
+                axis=0,
+            ),
             lax.all_gather(slot_dual, "tiles", axis=0, tiled=True),
         )
         adv_rows = jnp.dot(adv_onehot, adv_all, precision=highest)

time: 471 us -> 425 us (0.902)
  blocking collectives: 142 us -> 75.4 us
  starting transfers between devices: 0.08 us -> 18.2 us
    all_gather x2 -> x0, blocking collectives: 74.1 us -> none  [body(): lax.all_gather(adv_dual, 'tiles', axis=0, tiled=True)]
    all_to_all x0 -> x2, starting transfers between devices: none -> 18.2 us  [body(): lax.all_to_all(jnp.stack([adv_dual] * lax.axis_size('tiles')), 'tiles', 0...]
    all_gather x2, blocking collectives: 67.9 us -> 75.4 us  [body(): lax.all_gather(slot_dual, 'tiles', axis=0, tiled=True)]
  transfers between devices with their start and end apart: 2 -> 4, of which waited for: 2 -> 2; matrix products, arithmetic and copies ran while one was open for 0% -> 1% of each run, Pallas kernels for 0% -> 0%
where the time goes in v1:
time: 425 us; the launch traced here: 424 us
  waiting for transfers between devices  290 us (68%)
  blocking collectives  75.4 us (18%)
  starting transfers between devices  18.2 us (4%)
  other arithmetic  16.9 us (4%)
  between operations  14.1 us (3%)
  matrix products  7.15 us (2%)
    unnamed x4, waiting for transfers between devices  290 us
    all_gather x2, blocking collectives, body(): lax.all_gather(slot_dual, 'tiles', axis=0, tiled=True)  75.4 us
    all_to_all x2, starting transfers between devices, body(): lax.all_to_all(jnp.stack([adv_dual] * lax.axis_size('tiles')), 'tiles', 0...  18.2 us
  transfers between devices with their start and end apart: 4, of which 2 were waited for; matrix products, arithmetic and copies ran while one was open for 1% of the time, Pallas kernels for 0%

profile of v1, /device:TPU:1, one launch (start us, length us, event | category | flops | bytes accessed | tf_op | source)
XLA Modules:
  0.0 424.1 jit_solution(9012968819520928089)
XLA Ops:
  7.2 1.5 stack.4
  8.7 0.0 copy-start.3
  8.7 0.0 copy-start.4
  8.7 11.5 %all-to-all-start = ((f32[128,1,512]{2,1,0:T(1,128)}), f32[128,1,512]{2,1,0:T(1,128)S(1)}, u32[]{:S(2)}, u32[]{:S(2)}) async-start(f32[128,1,512]{2,1,0:T(1,128)} %stack.4), calls=%async_computation | async-start | bytes 524288 | tf_op jit(solution)/shard_map/all_to_all | solution.py:42
  20.2 0.0 all-reduce.11.cloned.1.call-start
  20.2 37.7 %all-gather = f32[128,1,1024]{2,1,0:T(1,128)S(1)} all-gather(f32[1,1,1024]{2,1,0:T(1,128)} %bitcast.49), channel_id=1, replica_groups=mesh['tiles'=128] {'tiles'}, dimensions={0}, use_global_device_ids=true | all-gather | bytes 528384 | tf_op jit(solution)/shard_map/all_gather | solution.py:45
  57.9 0.7 compare_convert_fusion
  58.6 0.7 convert_element_type.12
  59.3 0.1 copy.13
  59.4 1.0 fusion.16
  60.4 0.0 copy-start.5
  60.4 0.0 copy-start.6
  60.4 0.0 all-to-all-done
  60.4 0.9 fusion.22
  61.3 0.0 copy-start.1
  61.3 0.0 copy-start.2
  61.3 0.0 copy-start
  61.3 5.0 %fusion.26 = (f32[2,512]{1,0:T(2,128)S(1)}, f32[2,1024]{1,0:T(2,128)S(1)}) fusion(f32[2,512,1024]{2,1,0:T(8,128)} %param.9, f32[2]{0:T(128)S(1)} %compare_convert_fusion, f32[2,64,8]{2,1,0:T(8,128)S(1)} %copy.13, f32[2,1024]{1,0:T(2,128)S(1)} %fusion.16, f32[2,512]{1,0:T(2,128)S(1)} %fusion.22, bf16[2,512,1024]{2,1,0:T(8,128)(2,1)} %param.10), kind=kLoop, calls=%fused_computation.31 | loop fusion | flops 13628416 | bytes 6320136 | tf_op jit(solution)/shard_map/reduce_sum | solution.py:56
  66.3 0.0 copy-done.3
  66.3 1.1 fusion.42
  67.4 0.0 copy-done.4
  67.4 1.3 fusion.40
  68.7 0.0 all-reduce.11.cloned.1.call-update
  68.7 144.9 %all-reduce.11.cloned.1.call-done = (f32[128,1024]{1,0:T(8,128)}, f32[128,512]{1,0:T(8,128)}) async-done(((f32[128,1024]{1,0:T(8,128)}, f32[128,512]{1,0:T(8,128)}), (f32[128,1024]{1,0:T(8,128)}, f32[128,512]{1,0:T(8,128)})) %all-reduce.11.cloned.1.call-update) | async-done | bytes 786448
  213.6 0.0 copy-done.5
  213.6 0.0 copy-done.6
  213.6 0.7 fusion.37
  214.4 0.8 stack.5
  215.2 6.7 %all-to-all-start.1 = ((f32[128,1,512]{2,1,0:T(1,128)}), f32[128,1,512]{2,1,0:T(1,128)S(1)}, u32[]{:S(2)}, u32[]{:S(2)}) async-start(f32[128,1,512]{2,1,0:T(1,128)} %stack.5), calls=%async_computation.1 | async-start | bytes 524288 | tf_op jit(solution)/shard_map/all_to_all | solution.py:42
  221.9 0.0 all-reduce.9.cloned.1.call-start
  221.9 0.0 copy-done.1
  221.9 0.0 copy-done.2
  221.9 0.8 fusion.31
  222.7 37.7 %all-gather.1 = f32[128,1,1024]{2,1,0:T(1,128)S(1)} all-gather(f32[1,1,1024]{2,1,0:T(1,128)S(1)} %bitcast.47), channel_id=1, replica_groups=mesh['tiles'=128] {'tiles'}, dimensions={0}, use_global_device_ids=true | all-gather | bytes 528384 | tf_op jit(solution)/shard_map/all_gather | solution.py:45
  260.4 0.3 fusion.13
  260.7 0.0 all-to-all-done.1
  260.8 0.2 fusion.19
  261.0 0.0 copy-done
  261.0 6.4 %fusion.11 = (f32[2,1024]{1,0:T(2,128)S(1)}, f32[2,512]{1,0:T(2,128)S(1)}, f32[2,512,1024]{2,1,0:T(8,128)}) fusion(f32[2,1024]{1,0:T(2,128)S(1)} %fusion.16, f32[2,512]{1,0:T(2,128)S(1)} %fusion.22, bf16[2,512,1024]{2,1,0:T(8,128)(2,1)S(1)} %copy-done, f32[2,512,1024]{2,1,0:T(8,128)} %param.9, f32[2]{0:T(128)S(1)} %compare_convert_fusion, ...), kind=kLoop, calls=%fused_computation.16 | loop fusion | flops 19919872 | bytes 10526728 | tf_op jit(solution)/shard_map/reduce_sum | solution.py:57
  267.4 1.1 fusion.41
  268.5 1.3 fusion.39
  269.7 0.0 all-reduce.9.cloned.1.call-update
  269.8 144.9 %all-reduce.9.cloned.1.call-done = (f32[128,512]{1,0:T(8,128)}, f32[128,1024]{1,0:T(8,128)}) async-done(((f32[128,512]{1,0:T(8,128)}, f32[128,1024]{1,0:T(8,128)}), (f32[128,512]{1,0:T(8,128)}, f32[128,1024]{1,0:T(8,128)})) %all-reduce.9.cloned.1.call-update) | async-done | bytes 786448
  414.6 1.3 fusion.38
  415.9 1.4 fusion.32
Async XLA Ops:
  8.7 57.6 %copy-start.3 = (s32[2]{0:T(128)S(1)}, s32[2]{0:T(128)}, u32[]{:S(2)}) copy-start(s32[2]{0:T(128)} %param.12) | copy-start | bytes 28
  8.7 58.7 %copy-start.4 = (s32[2]{0:T(128)S(1)}, s32[2]{0:T(128)}, u32[]{:S(2)}) copy-start(s32[2]{0:T(128)} %param.13) | copy-start | bytes 28
  8.7 51.7 %all-to-all-start = ((f32[128,1,512]{2,1,0:T(1,128)}), f32[128,1,512]{2,1,0:T(1,128)S(1)}, u32[]{:S(2)}, u32[]{:S(2)}) async-start(f32[128,1,512]{2,1,0:T(1,128)} %stack.4), calls=%async_computation | async-start | bytes 524288 | tf_op jit(solution)/shard_map/all_to_all | solution.py:42
  20.2 193.4 %all-reduce.11.cloned.1.call-start = ((), (), s32[]{:S(2)}) async-start(), calls=%async_computation.3 | async-start | bytes 1572864
  60.4 153.3 %copy-start.5 = (f32[1,512]{1,0:T(1,128)S(1)}, f32[1,512]{1,0:T(1,128)}, u32[]{:S(2)}) copy-start(f32[1,512]{1,0:T(1,128)} %param.14) | copy-start | bytes 6148
  60.4 153.2 %copy-start.6 = (f32[1,512]{1,0:T(1,128)S(1)}, f32[1,512]{1,0:T(1,128)}, u32[]{:S(2)}) copy-start(f32[1,512]{1,0:T(1,128)} %param.16) | copy-start | bytes 6148
  61.3 160.7 %copy-start.1 = (f32[1,1024]{1,0:T(1,128)S(1)}, f32[1,1024]{1,0:T(1,128)}, u32[]{:S(2)}) copy-start(f32[1,1024]{1,0:T(1,128)} %param.15) | copy-start | bytes 12292
  61.3 160.7 %copy-start.2 = (f32[1,1024]{1,0:T(1,128)S(1)}, f32[1,1024]{1,0:T(1,128)}, u32[]{:S(2)}) copy-start(f32[1,1024]{1,0:T(1,128)} %param.17) | copy-start | bytes 12292
  61.3 199.7 %copy-start = (bf16[2,512,1024]{2,1,0:T(8,128)(2,1)S(1)}, bf16[2,512,1024]{2,1,0:T(8,128)(2,1)}, u32[]{:S(2)}) copy-start(bf16[2,512,1024]{2,1,0:T(8,128)(2,1)} %param.10) | copy-start | bytes 6291460
  215.2 45.6 %all-to-all-start.1 = ((f32[128,1,512]{2,1,0:T(1,128)}), f32[128,1,512]{2,1,0:T(1,128)S(1)}, u32[]{:S(2)}, u32[]{:S(2)}) async-start(f32[128,1,512]{2,1,0:T(1,128)} %stack.5), calls=%async_computation.1 | async-start | bytes 524288 | tf_op jit(solution)/shard_map/all_to_all | solution.py:42
  221.9 192.8 %all-reduce.9.cloned.1.call-start = ((), (), s32[]{:S(2)}) async-start(), calls=%async_computation.2 | async-start | bytes 1572864
Sparse Core Ops, SparseCore 0:
  68.8 144.7 all-reduce.10
  269.9 144.7 all-reduce.8
